TPU v7x, 32 devices: a whole 2x2x4 slice. The times are simulated.
32 devices in a mesh: gx: 4 (over z), gy: 4 (over y, x), gz: 2 (over core).
Axes of the slice: x: 2, y: 2, z: 4, core: 2. Of those that a mesh axis runs over, the one named last changes fastest.
Arguments:
- positions: float32 [3, 4096], P(None, ('gx', 'gy', 'gz')), may hold values from 0 to 4.5
- species: int32 [4096], P(('gx', 'gy', 'gz')), may hold values from 0 to 88
- cell_map: int32 [32, 128], P(('gx', 'gy', 'gz')), may hold values from 0 to 127, each once within a row
- neighbours: int32 [8, 4096], P(None, ('gx', 'gy', 'gz')), may hold values from 0 to 511
- struct_ids: int32 [4096], P(('gx', 'gy', 'gz')), may hold values from 0 to 15, as said below
- embed: float32 [89, 128], replicated, may hold values from -6 to 6
- w_up: float32 [2, 128, 128], replicated, may hold values from -0.5 to 0.5
- w_rad_in: float32 [2, 8, 64], replicated, may hold values from -2 to 2
- w_rad_out: float32 [2, 64, 256], replicated, may hold values from -0.75 to 0.75
- w_mix: float32 [2, 3, 128, 128], replicated, may hold values from -0.5 to 0.5
- read_first: float32 [128], replicated, may hold values from -0.5 to 0.5
- read_hidden: float32 [128, 16], replicated, may hold values from -0.5 to 0.5
- read_last: float32 [16], replicated, may hold values from -1.5 to 1.5
Outputs:
- energies: float32 [16], replicated
- virials: float32 [9, 16], replicated
- forces: float32 [3, 4096], P(None, ('gx', 'gy', 'gz'))
Inputs may be any that keep to these rules, and one draw needn't show every extreme that they name: `cell_map`: each row is a permutation. `neighbours`: entries index the extended rows of the atom's own device. `struct_ids`: atoms of the devices with gx index a have ids from a * 4 to (a + 1) * 4 - 1.
All inputs are finite; a program needn't handle non-finite values.
Results may differ from a plain program's by a relative error of at most 0.0003.
Values sent between devices are 32-bit elements; how exact they have to be, the bound alone decides.
A program may use at most 64 MiB of HBM per device.

v0:
```python
import functools
import math

import jax
import jax.numpy as jnp
from jax import lax
from jax.experimental import pallas as pl
from jax.experimental.pallas import tpu as pltpu
from jax.sharding import PartitionSpec as P

SLAB_STRUCTS = 4
AXES = ("gx", "gy", "gz")
MESH = pl.DeviceIdType.MESH
cutoff = 6.0
box_side = 4.5
soften = 0.25
f32 = jnp.float32
bf16 = jnp.bfloat16


def split2(x):
    high = x.astype(bf16)
    return high, (x - high.astype(f32)).astype(bf16)


def parts3(x):
    high = x.astype(bf16).astype(f32)
    rest = x - high
    mid = rest.astype(bf16).astype(f32)
    return jnp.concatenate([high, mid, rest - mid], axis=0)


def dot(left, right, dims):
    return lax.dot_general(
        left, right, (((dims[0],), (dims[1],)), ((), ())), preferred_element_type=f32
    )


def dot3(left, right, dims):
    lh, ll = split2(left)
    rh, rl = split2(right)
    return dot(lh, rh, dims) + (dot(lh, rl, dims) + dot(ll, rh, dims))


def dot3_tall(left, right):
    lh = left.astype(bf16).astype(f32)
    rh = right.astype(bf16).astype(f32)
    lefts = jnp.concatenate([lh, lh, left - lh], axis=0).astype(bf16)
    rights = jnp.concatenate([rh, right - rh, rh], axis=0).astype(bf16)
    return dot(lefts, rights, (0, 0))


def pick(table, chosen):
    width = table.shape[0]
    both = dot(jnp.concatenate(split2(table), axis=0), chosen, (1, 0))
    return both[:width] + both[width:]


def to_col(row):
    n = row.shape[1]
    same = lax.broadcasted_iota(jnp.int32, (n, n), 0) == lax.broadcasted_iota(jnp.int32, (n, n), 1)
    return jnp.sum(jnp.where(same, jnp.broadcast_to(row, (n, n)), 0.0), axis=1, keepdims=True)


def sigmoid(x):
    return 1.0 / (1.0 + jnp.exp(-x))


def sin_cos_pi(turns):
    near = jnp.floor(turns + 0.5)
    x = (turns - near) * math.pi
    sign = 1.0 - 2.0 * (near - 2.0 * jnp.floor(near * 0.5))
    x2 = x * x
    s = jnp.full_like(x, 1.0 / math.factorial(13))
    for p in (11, 9, 7, 5, 3, 1):
        s = s * x2 + (-1.0) ** ((p - 1) // 2) / math.factorial(p)
    c = jnp.full_like(x, 1.0 / math.factorial(12))
    for p in (10, 8, 6, 4, 2, 0):
        c = c * x2 + (-1.0) ** (p // 2) / math.factorial(p)
    return s * x * sign, c * sign


def kernel(
    counts,
    pos, spe, cmap, nbr, sid, embed, w_up, w_ri, w_ro, w_mix, rfirst, rhid, rlast,
    en_out, vir_out, f_out,
    stage, emb, oh, soh, dirs, pre, rad, picked, grads, d_rad, d_pick, ddir, feats,
    sendp, sends, recvp, reccs, lsend, tables, back, backs, fsend, frecv, red, redstage,
    slab_buf, gx_send, gx_buf,
    p_s, p_r, s_s, s_r, l_s, l_r, b_s, b_r, f_s, f_r, a_s, a_r, g_s, g_r,
):
    nx, ny, nz = counts
    size = dict(zip(AXES, counts))
    me = {axis: lax.axis_index(axis) for axis in AXES}
    atoms = pos.shape[1]
    neigh = nbr.shape[0]
    edges = neigh * atoms
    chans = embed.shape[1]
    per_cell = atoms // 8
    scaling = 1.0 / math.sqrt(neigh)

    def at(shift):
        return {
            axis: lax.rem(me[axis] + (step % size[axis]), size[axis])
            for axis, step in zip(AXES, shift)
            if step % size[axis]
        }

    slab_shifts = [(0, j, k) for j in range(ny) for k in range(nz) if (j, k) != (0, 0)]
    gx_shifts = [(i, 0, 0) for i in range(1, nx)]
    peers = slab_shifts + gx_shifts
    barrier = pltpu.get_barrier_semaphore()
    for shift in peers:
        pl.semaphore_signal(barrier, inc=1, device_id=at(shift), device_id_type=MESH)

    def face_shift(axis, step):
        return tuple(step if a == axis else 0 for a in range(3))

    def remote(src, dst, send, recv, shift):
        return pltpu.make_async_remote_copy(
            src_ref=src, dst_ref=dst, send_sem=send, recv_sem=recv,
            device_id=at(shift), device_id_type=MESH,
        )

    stage[...] = jnp.zeros_like(stage)
    stage[0:neigh, :] = nbr[...].astype(f32)
    base = stage.shape[0] - 8
    stage[base : base + 3, :] = pos[...]
    stage[base + 3 : base + 4, :] = spe[...].astype(f32)
    stage[base + 4 : base + 5, :] = sid[...].astype(f32)
    iota0 = lax.broadcasted_iota(jnp.int32, (atoms, atoms), 0)
    iota1 = lax.broadcasted_iota(jnp.int32, (atoms, atoms), 1)
    cm_row = cmap[...]
    order_t = jnp.where(iota0 == cm_row, 1.0, 0.0).astype(bf16)
    height = stage.shape[0]
    moved = dot(parts3(stage[...]).astype(bf16), order_t, (1, 0))
    moved = moved[:height] + moved[height : 2 * height] + moved[2 * height :]
    nbr_c = moved[0:neigh].astype(jnp.int32)
    tail = moved[base : base + 8]
    row8 = lax.broadcasted_iota(jnp.int32, (8, atoms), 0)
    pos_c = jnp.where(row8 < 3, tail, 0.0)
    spe_c = tail[3:4].astype(jnp.int32)
    sid_c = tail[4:5].astype(jnp.int32)
    sendp[...] = pos_c
    sends[...] = jnp.broadcast_to(spe_c, (8, atoms))

    pl.semaphore_wait(barrier, len(peers))
    copies = []
    for axis in range(3):
        for face, step in ((2 * axis, 1), (2 * axis + 1, -1)):
            copies.append(remote(sendp, recvp.at[face], p_s.at[face], p_r.at[face], face_shift(axis, step)))
            copies.append(remote(sends, reccs.at[face], s_s.at[face], s_r.at[face], face_shift(axis, step)))
    for copy in copies:
        copy.start()

    cm_col = to_col(cm_row.astype(f32)).astype(jnp.int32)
    own_slot = jnp.broadcast_to(cm_col, (atoms, atoms))
    half = atoms // 2
    bits = [(iota0 // (per_cell * w)) % 2 for w in (4, 2, 1)]
    inner = iota0 % per_cell
    ids = [own_slot]
    for axis in range(3):
        others = [bits[a] for a in range(3) if a != axis]
        ids.append(
            (axis + 1) * atoms + (1 - bits[axis]) * half
            + others[0] * (2 * per_cell) + others[1] * per_cell + inner
        )
    for t in range(4):
        for k in range(neigh):
            oh[t * atoms : (t + 1) * atoms, k * atoms : (k + 1) * atoms] = jnp.where(
                ids[t] == nbr_c[k : k + 1], 1.0, 0.0
            ).astype(bf16)
    elements = embed.shape[0]
    emb[...] = jnp.zeros_like(emb)
    emb[0:elements, :] = embed[...]
    table = emb[...]
    lifted_zero = dot3(table, w_up[0], (1, 0)).T
    el_iota = lax.broadcasted_iota(jnp.int32, (table.shape[0], atoms), 0)
    own_el = jnp.where(el_iota == spe_c, 1.0, 0.0).astype(bf16)
    initial = pick(table.T, own_el)
    first_col = to_col(rfirst[...])
    last_col = to_col(rlast[...])

    for copy in copies:
        copy.wait()

    lane_bits = [(lax.broadcasted_iota(jnp.int32, (8, atoms), 1) // (per_cell * w)) % 2 for w in (4, 2, 1)]
    pieces = [jnp.where(row8 == 3, jnp.broadcast_to(spe_c, (8, atoms)).astype(f32), pos_c)]
    for axis in range(3):
        low = lane_bits[axis] == 1
        where_pos = jnp.where(low, recvp[2 * axis], recvp[2 * axis + 1])
        shifted = where_pos + jnp.where(low, -box_side, box_side)
        where_pos = jnp.where(row8 == axis, shifted, where_pos)
        where_el = jnp.where(low, reccs[2 * axis], reccs[2 * axis + 1]).astype(f32)
        pieces.append(jnp.where(row8 == 3, where_el, where_pos))
    ext = jnp.concatenate(pieces, axis=1)
    ext3 = jnp.concatenate([parts3(ext), jnp.zeros_like(ext)], axis=0).astype(bf16)
    far = dot(ext3, oh[...], (1, 0))
    far = far[0:8] + far[8:16] + far[16:24]
    ev = far - jnp.concatenate([pos_c] * neigh, axis=1)
    far_el = far[3:4].astype(jnp.int32)
    for k in range(neigh):
        cols = slice(k * atoms, (k + 1) * atoms)
        soh[:, cols] = jnp.where(el_iota == far_el[:, cols], 1.0, 0.0).astype(bf16)
    r2 = ev[0:1] * ev[0:1] + ev[1:2] * ev[1:2] + ev[2:3] * ev[2:3]
    radius = jnp.sqrt(r2 + soften)
    inv = 1.0 / radius
    room = jnp.maximum(0.0, 1.0 - radius * radius / (cutoff * cutoff))
    env = room * room
    d_env = room * radius * (-4.0 / (cutoff * cutoff))
    bessels = w_ri.shape[1]
    harm = (lax.broadcasted_iota(jnp.int32, (bessels, edges), 0) + 1).astype(f32)
    sn, cs = sin_cos_pi(harm * (radius * (1.0 / cutoff)))
    amp = math.sqrt(2.0 / cutoff) * inv
    bessel = sn * (amp * env)
    d_bessel = amp * (env * (harm * (math.pi / cutoff) * cs - sn * inv) + sn * d_env)
    dirs[...] = ev * inv

    chunk = 32

    def radial(layer):
        x = dot3_tall(w_ri[layer], bessel)
        pre[layer] = x
        rad[layer] = dot3_tall(w_ro[layer], x * sigmoid(x))

    def forward(layer):
        for c in range(0, chans, chunk):
            s = v0 = v1 = v2 = None
            for k in range(neigh):
                cols = pl.ds(k * atoms, atoms)
                p = picked[layer, pl.ds(c, chunk), cols]
                a = rad[layer, pl.ds(c, chunk), cols] * p
                b = rad[layer, pl.ds(chans + c, chunk), cols] * p
                d = [dirs[pl.ds(m, 1), cols] for m in range(3)]
                if k == 0:
                    s, v0, v1, v2 = a, d[0] * b, d[1] * b, d[2] * b
                else:
                    s, v0, v1, v2 = s + a, v0 + d[0] * b, v1 + d[1] * b, v2 + d[2] * b
            s = s * scaling
            vs = [v * scaling for v in (v0, v1, v2)]
            rows = pl.ds(c, chunk)
            for m in range(3):
                feats[layer, 3 + m, rows, :] = vs[m]
            feats[layer, 0, rows, :] = s
            feats[layer, 1, rows, :] = vs[0] * vs[0] + vs[1] * vs[1] + vs[2] * vs[2]
            feats[layer, 2, rows, :] = s * s
        stacked = feats[layer, 0:3].reshape(3 * chans, atoms)
        return dot3(w_mix[layer].reshape(3 * chans, chans), stacked, (0, 0))

    def backward(layer, d_mix, with_pick):
        d_st = dot3(w_mix[layer].reshape(3 * chans, chans), d_mix, (1, 0))
        d_s = d_st[0:chans] + 2.0 * feats[layer, 0] * d_st[2 * chans :]
        grads[0] = d_s * scaling
        twice = d_st[chans : 2 * chans] * (2.0 * scaling)
        for m in range(3):
            grads[1 + m] = feats[layer, 3 + m] * twice
        for k in range(neigh):
            cols = pl.ds(k * atoms, atoms)
            d = [dirs[pl.ds(m, 1), cols] for m in range(3)]
            acc = [jnp.zeros((8, atoms), f32)] * 3
            for c in range(0, chans, chunk):
                rows = pl.ds(c, chunk)
                g = [grads[m, rows, :] for m in range(4)]
                p = picked[layer, rows, cols]
                b = rad[layer, pl.ds(chans + c, chunk), cols]
                t = d[0] * g[1] + d[1] * g[2] + d[2] * g[3]
                d_rad[rows, cols] = g[0] * p
                d_rad[pl.ds(chans + c, chunk), cols] = t * p
                if with_pick:
                    d_pick[rows, cols] = g[0] * rad[layer, rows, cols] + t * b
                q = b * p
                acc = [
                    acc[m] + jnp.sum((g[1 + m] * q).reshape(chunk // 8, 8, atoms), axis=0)
                    for m in range(3)
                ]
            for m in range(3):
                ddir[layer, pl.ds(m, 1), cols] = jnp.sum(acc[m], axis=0, keepdims=True)

    def backward_radial(layer):
        d_hidden = dot3(w_ro[layer], d_rad[...], (1, 0))
        x = pre[layer]
        sig = sigmoid(x)
        return dot3(w_ri[layer], d_hidden * sig * (1.0 + x * (1.0 - sig)), (1, 0))

    ddir[...] = jnp.zeros_like(ddir)
    radial(0)
    picked[0] = pick(lifted_zero, soh[...])
    layer_out = initial + forward(0)
    lifted = dot3(layer_out, w_up[1], (0, 0))
    grid = (2, 2, 2, per_cell, chans)
    lsend[...] = lifted.reshape(grid)

    def part(ref, axis, side):
        return ref.at[(slice(None),) * axis + (side,)]

    copies = []
    for axis in range(3):
        for side, step in ((1, 1), (0, -1)):
            i = 2 * axis + side
            copies.append(
                remote(part(lsend, axis, side), part(tables.at[axis], axis, side), l_s.at[i], l_r.at[i], face_shift(axis, step))
            )
    for copy in copies:
        copy.start()
    radial(1)
    own_pick = pick(lifted.T, oh[0:atoms, :])
    for copy in copies:
        copy.wait()
    ghosts = jnp.concatenate([tables[a].reshape(atoms, chans).T for a in range(3)], axis=1)
    picked[1] = own_pick + pick(ghosts, oh[atoms:, :])
    second = layer_out + forward(1)
    x2 = dot3(rhid[...], second, (0, 0))
    sig2 = sigmoid(x2)
    energy = jnp.sum(first_col * layer_out, axis=0, keepdims=True) + jnp.sum(
        last_col * (x2 * sig2), axis=0, keepdims=True
    )
    d_second = dot3(rhid[...], last_col * (sig2 * (1.0 + x2 * (1.0 - sig2))), (1, 0))
    backward(1, d_second, True)
    d_ext = dot(oh[...], jnp.concatenate(split2(d_pick[...]), axis=0), (1, 1))
    d_ext = d_ext[:, :chans] + d_ext[:, chans:]
    for axis in range(3):
        back[axis] = d_ext[(axis + 1) * atoms : (axis + 2) * atoms].reshape(grid)
    copies = []
    for axis in range(3):
        for side, step in ((1, -1), (0, 1)):
            i = 2 * axis + side
            copies.append(
                remote(part(back.at[axis], axis, side), part(backs.at[axis], axis, side), b_s.at[i], b_r.at[i], face_shift(axis, step))
            )
    for copy in copies:
        copy.start()
    d_bes = backward_radial(1)
    for copy in copies:
        copy.wait()
    d_lifted = d_ext[0:atoms]
    for axis in range(3):
        d_lifted = d_lifted + backs[axis].reshape(atoms, chans)
    d_layer = d_second + first_col + dot3(w_up[1], d_lifted, (1, 1))
    backward(0, d_layer, False)
    d_bes = d_bes + backward_radial(0)
    d_dir = ddir[0] + ddir[1]
    along = d_dir * ev
    d_radius = jnp.sum(d_bes * d_bessel, axis=0, keepdims=True) - (
        along[0:1] + along[1:2] + along[2:3]
    ) * (inv * inv)
    edge_row = lax.broadcasted_iota(jnp.int32, (8, edges), 0)
    eg = jnp.where(edge_row < 3, d_dir * inv + ev * (d_radius * inv), 0.0)

    redstage[...] = jnp.zeros_like(redstage)

    def over_slots(x):
        total = x[:, 0:atoms]
        for k in range(1, neigh):
            total = total + x[:, k * atoms : (k + 1) * atoms]
        return total

    for r in range(3):
        redstage[3 * r : 3 * r + 3, :] = -over_slots(ev[r : r + 1] * eg)[0:3]
    redstage[9:10, :] = energy
    structs = SLAB_STRUCTS * nx
    member = jnp.where(
        lax.broadcasted_iota(jnp.int32, (structs, atoms), 0) == sid_c, 1.0, 0.0
    ).astype(bf16)
    shares = dot(parts3(redstage[...]).astype(bf16), member, (1, 1))
    shares = shares[0:16] + shares[16:32] + shares[32:48]
    red[...] = shares
    my_slot = me["gy"] * nz + me["gz"]
    sums = []
    for i, shift in enumerate(slab_shifts):
        sums.append(remote(red, slab_buf.at[my_slot], a_s.at[i], a_r.at[i], shift))
    for copy in sums:
        copy.start()

    eg3 = jnp.concatenate([parts3(eg), jnp.zeros_like(eg)], axis=0).astype(bf16)
    spread = dot(eg3, oh[...], (1, 1))
    spread = spread[0:8] + spread[8:16] + spread[16:24]
    for axis in range(3):
        fsend[axis] = spread[:, (axis + 1) * atoms : (axis + 2) * atoms]
    copies = []
    for axis in range(3):
        for face, step in ((2 * axis, -1), (2 * axis + 1, 1)):
            copies.append(remote(fsend.at[axis], frecv.at[face], f_s.at[face], f_r.at[face], face_shift(axis, step)))
    for copy in copies:
        copy.start()
    own = spread[:, 0:atoms] - over_slots(eg)
    slab_buf[my_slot] = red[...]
    for copy in sums:
        copy.wait()
    total = slab_buf[0]
    for i in range(1, ny * nz):
        total = total + slab_buf[i]
    gx_send[...] = total
    sums = []
    for i, shift in enumerate(gx_shifts):
        sums.append(remote(gx_send, gx_buf.at[i], g_s.at[i], g_r.at[i], shift))
    for copy in sums:
        copy.start()
    for copy in copies:
        copy.wait()
    for axis in range(3):
        own = own + jnp.where(lane_bits[axis] == 1, frecv[2 * axis], frecv[2 * axis + 1])
    order = jnp.where(own_slot == iota1, 1.0, 0.0).astype(bf16)
    own3 = jnp.concatenate([parts3(-own), jnp.zeros_like(own)], axis=0).astype(bf16)
    forces = dot(own3, order, (1, 0))
    f_out[...] = (forces[0:8] + forces[8:16] + forces[16:24])[0:3]
    for copy in sums:
        copy.wait()
    for i in range(len(gx_shifts)):
        total = total + gx_buf[i]
    vir_out[...] = total[0:9]
    en_out[...] = total[9:10]


def shards(counts, *args):
    (positions, species, cell_map, neighbours, struct_ids, embed, w_up, w_rad_in, w_rad_out,
     w_mix, read_first, read_hidden, read_last) = args
    nx, ny, nz = counts
    atoms = positions.shape[1]
    neigh = neighbours.shape[0]
    edges = neigh * atoms
    chans = embed.shape[1]
    hidden = w_rad_in.shape[2]
    per_cell = atoms // 8
    structs = SLAB_STRUCTS * nx
    el_rows = -(-embed.shape[0] // 128) * 128
    grid = (2, 2, 2, per_cell, chans)
    dma = pltpu.SemaphoreType.DMA
    vm = lambda *shape: pltpu.VMEM(shape, f32)
    vmem = pl.BlockSpec(memory_space=pltpu.VMEM)
    energies, virials, forces = pl.pallas_call(
        functools.partial(kernel, counts),
        out_shape=(
            jax.ShapeDtypeStruct((1, structs), f32),
            jax.ShapeDtypeStruct((9, structs), f32),
            jax.ShapeDtypeStruct((3, atoms), f32),
        ),
        in_specs=[vmem] * 13,
        out_specs=(vmem, vmem, vmem),
        scratch_shapes=[
            vm(-(-neigh // 8) * 8 + 8, atoms),
            vm(el_rows, chans),
            pltpu.VMEM((4 * atoms, edges), bf16),
            pltpu.VMEM((el_rows, edges), bf16),
            vm(8, edges),
            vm(2, hidden, edges),
            vm(2, 2 * chans, edges),
            vm(2, chans, edges),
            vm(4, chans, atoms),
            vm(2 * chans, edges),
            vm(chans, edges),
            vm(2, 8, edges),
            vm(2, 6, chans, atoms),
            vm(8, atoms),
            pltpu.VMEM((8, atoms), jnp.int32),
            vm(6, 8, atoms),
            pltpu.VMEM((6, 8, atoms), jnp.int32),
            vm(*grid),
            vm(3, *grid),
            vm(3, *grid),
            vm(3, *grid),
            vm(3, 8, atoms),
            vm(6, 8, atoms),
            vm(16, structs),
            vm(16, atoms),
            vm(ny * nz, 16, structs),
            vm(16, structs),
            vm(max(nx - 1, 1), 16, structs),
        ]
        + [dma((6,))] * 10
        + [dma((ny * nz - 1,))] * 2
        + [dma((max(nx - 1, 1),))] * 2,
        compiler_params=pltpu.CompilerParams(
            collective_id=0, has_side_effects=True, vmem_limit_bytes=48 * 1024 * 1024
        ),
    )(
        positions, species[None], cell_map, neighbours, struct_ids[None], embed, w_up,
        w_rad_in, w_rad_out, w_mix, read_first[None], read_hidden, read_last[None],
    )
    return energies[0], virials, forces


def solution(mesh):
    counts = tuple(mesh.shape[axis] for axis in AXES)
    return jax.shard_map(
        functools.partial(shards, counts),
        mesh=mesh,
        in_specs=(P(None, AXES), P(AXES), P(AXES, None), P(None, AXES), P(AXES))
        + (P(),) * 8,
        out_specs=(P(), P(), P(None, AXES)),
        check_vma=False,
    )
```

profile of v0, /device:TPU:0, one launch (start us, length us, event | category | flops | bytes accessed | tf_op | source)
XLA Modules:
  0.0 36.1 jit_solution(8321136316924379487)
XLA Ops:
  0.6 0.0 copy-start.3
  0.6 0.0 copy-start.4
  0.7 0.0 copy-start.5
  0.7 0.0 copy-start.6
  0.7 0.0 copy-start.7
  0.7 0.0 copy-start.8
  0.7 0.0 copy-start.9
  0.7 0.0 copy-start.10
  0.7 0.0 copy-start.11
  0.7 0.9 %copy.16.rhid = f32[128,16]{1,0:T(8,128)S(1)} copy(f32[128,16]{0,1:T(8,128)} %param.24) | data formatting | bytes 16384 | tf_op args[11]
  1.6 0.0 copy-done.3
  1.6 0.0 copy-done.4
  1.6 0.0 copy-done.5
  1.6 0.0 copy-done.6
  1.6 0.0 copy-done.7
  1.6 0.0 copy-done.8
  1.6 0.0 copy-done.9
  1.6 0.0 copy-done.10
  1.7 0.0 copy-done.11
  1.7 0.0 copy-start
  1.7 1.0 %copy-done = f32[2,3,128,128]{3,2,1,0:T(8,128)S(1)} copy-done((f32[2,3,128,128]{3,2,1,0:T(8,128)S(1)}, f32[2,3,128,128]{3,2,1,0:T(8,128)}, u32[]{:S(2)}) %copy-start) | copy-done | bytes 393240
  2.7 0.0 copy-start.1
  2.7 0.9 %copy-done.1 = f32[2,128,128]{2,1,0:T(8,128)S(1)} copy-done((f32[2,128,128]{2,1,0:T(8,128)S(1)}, f32[2,128,128]{2,1,0:T(8,128)}, u32[]{:S(2)}) %copy-start.1) | copy-done | bytes 131096
  3.6 0.0 copy-start.2
  3.6 0.9 %copy-done.2 = f32[2,64,256]{2,1,0:T(8,128)S(1)} copy-done((f32[2,64,256]{2,1,0:T(8,128)S(1)}, f32[2,64,256]{2,1,0:T(8,128)}, u32[]{:S(2)}) %copy-start.2) | copy-done | bytes 131096
  4.5 29.9 %shard_map.148 = (f32[1,16]{1,0:T(1,128)S(1)}, f32[9,16]{1,0:T(8,128)S(1)}, f32[3,128]{1,0:T(4,128)S(1)}) custom-call(f32[3,128]{1,0:T(4,128)S(1)} %copy-done.6, s32[1,128]{1,0:T(1,128)S(1)} %bitcast.5, s32[1,128]{1,0:T(1,128)S(1)} %copy-done.8, s32[8,128]{1,0:T(8,128)S(1)} %copy-done.5, s32[1,128]{1,0:T(1,128)S(1)} %bitcast.6, f32[89,128]{1,0:T(8,128)S(1)} %copy-done.3, ...), custom_call_target="tpu_custom_call" | custom-call | tf_op jit(solution)/shard_map/pallas_call | solution.py:430
  34.4 0.5 %copy.20 = f32[16]{0:T(128)} copy(f32[16]{0:T(128)S(1)} %bitcast.9) | data formatting | bytes 128
  34.9 0.6 %copy.21 = f32[9,16]{1,0:T(8,128)} copy(f32[9,16]{1,0:T(8,128)S(1)} %get-tuple-element.13) | data formatting | bytes 1152
  35.5 0.6 %copy.22 = f32[3,128]{1,0:T(4,128)} copy(f32[3,128]{1,0:T(4,128)S(1)} %get-tuple-element.14) | data formatting | bytes 3072
Async XLA Ops:
  0.6 0.9 %copy-start.3 = (f32[89,128]{1,0:T(8,128)S(1)}, f32[89,128]{1,0:T(8,128)}, u32[]{:S(2)}) copy-start(f32[89,128]{1,0:T(8,128)} %embed.1) | copy-start | bytes 136708
  0.6 0.9 %copy-start.4 = (f32[2,8,64]{2,1,0:T(8,128)S(1)}, f32[2,8,64]{2,1,0:T(8,128)}, u32[]{:S(2)}) copy-start(f32[2,8,64]{2,1,0:T(8,128)} %w_ri.1) | copy-start | bytes 12292
  0.7 0.9 %copy-start.5 = (s32[8,128]{1,0:T(8,128)S(1)}, s32[8,128]{1,0:T(8,128)}, u32[]{:S(2)}) copy-start(s32[8,128]{1,0:T(8,128)} %nbr.1) | copy-start | bytes 12292
  0.7 0.9 %copy-start.6 = (f32[3,128]{1,0:T(4,128)S(1)}, f32[3,128]{1,0:T(4,128)}, u32[]{:S(2)}) copy-start(f32[3,128]{1,0:T(4,128)} %pos.1) | copy-start | bytes 4612
  0.7 0.9 %copy-start.7 = (s32[128]{0:T(128)S(1)}, s32[128]{0:T(128)}, u32[]{:S(2)}) copy-start(s32[128]{0:T(128)} %param.14) | copy-start | bytes 1540
  0.7 0.9 %copy-start.8 = (s32[1,128]{1,0:T(1,128)S(1)}, s32[1,128]{1,0:T(1,128)}, u32[]{:S(2)}) copy-start(s32[1,128]{1,0:T(1,128)} %cmap.1) | copy-start | bytes 1540
  0.7 0.9 %copy-start.9 = (s32[128]{0:T(128)S(1)}, s32[128]{0:T(128)}, u32[]{:S(2)}) copy-start(s32[128]{0:T(128)} %param.17) | copy-start | bytes 1540
  0.7 0.9 %copy-start.10 = (f32[128]{0:T(128)S(1)}, f32[128]{0:T(128)}, u32[]{:S(2)}) copy-start(f32[128]{0:T(128)} %param.23) | copy-start | bytes 1540
  0.7 0.9 %copy-start.11 = (f32[16]{0:T(128)S(1)}, f32[16]{0:T(128)}, u32[]{:S(2)}) copy-start(f32[16]{0:T(128)} %param.25) | copy-start | bytes 196
  1.7 1.0 %copy-start = (f32[2,3,128,128]{3,2,1,0:T(8,128)S(1)}, f32[2,3,128,128]{3,2,1,0:T(8,128)}, u32[]{:S(2)}) copy-start(f32[2,3,128,128]{3,2,1,0:T(8,128)} %w_mix.1) | copy-start | bytes 1179652
  2.7 0.9 %copy-start.1 = (f32[2,128,128]{2,1,0:T(8,128)S(1)}, f32[2,128,128]{2,1,0:T(8,128)}, u32[]{:S(2)}) copy-start(f32[2,128,128]{2,1,0:T(8,128)} %w_up.1) | copy-start | bytes 393220
  3.6 0.9 %copy-start.2 = (f32[2,64,256]{2,1,0:T(8,128)S(1)}, f32[2,64,256]{2,1,0:T(8,128)}, u32[]{:S(2)}) copy-start(f32[2,64,256]{2,1,0:T(8,128)} %w_ro.1) | copy-start | bytes 393220
where the time goes:
time: 36.3 us; the launch traced here: 36.1 us
  Pallas kernels  29.9 us (82%)
  local copies, waits for them, and re-layouts  5.38 us (15%)
  between operations  0.79 us (2%)
    pallas_call x1, Pallas kernels, shards(): pl.pallas_call(functools.partial(kernel, counts), out_shape=(jax.ShapeDty...  29.9 us
    unnamed x28, local copies, waits for them, and re-layouts  5.38 us

commit v1 on v0

--- a/solution.py
+++ b/solution.py
@@ -82,13 +82,25 @@
 
 def kernel(
     counts,
-    pos, spe, cmap, nbr, sid, embed, w_up, w_ri, w_ro, w_mix, rfirst, rhid, rlast,
+    *refs,
+):
+    inputs, outer = refs[:13], refs[13:]
+    run(counts, inputs, *outer)
+
+
+def run(
+    counts, inputs,
     en_out, vir_out, f_out,
     stage, emb, oh, soh, dirs, pre, rad, picked, grads, d_rad, d_pick, ddir, feats,
     sendp, sends, recvp, reccs, lsend, tables, back, backs, fsend, frecv, red, redstage,
     slab_buf, gx_send, gx_buf,
+    pos, spe, cmap, nbr, sid, embed, w_up, w_ri, w_ro, w_mix, rfirst, rhid, rlast, in_s,
     p_s, p_r, s_s, s_r, l_s, l_r, b_s, b_r, f_s, f_r, a_s, a_r, g_s, g_r,
 ):
+    held = (pos, spe, cmap, nbr, sid, embed, w_up, w_ri, w_ro, w_mix, rfirst, rhid, rlast)
+    loads = [pltpu.make_async_copy(src, dst, in_s.at[i]) for i, (src, dst) in enumerate(zip(inputs, held))]
+    for i in (3, 0, 1, 2, 4, 5, 6, 9, 8, 7, 10, 11, 12):
+        loads[i].start()
     nx, ny, nz = counts
     size = dict(zip(AXES, counts))
     me = {axis: lax.axis_index(axis) for axis in AXES}
@@ -123,6 +135,8 @@
         )
 
     stage[...] = jnp.zeros_like(stage)
+    for load in loads[:5]:
+        load.wait()
     stage[0:neigh, :] = nbr[...].astype(f32)
     base = stage.shape[0] - 8
     stage[base : base + 3, :] = pos[...]
@@ -170,6 +184,8 @@
             oh[t * atoms : (t + 1) * atoms, k * atoms : (k + 1) * atoms] = jnp.where(
                 ids[t] == nbr_c[k : k + 1], 1.0, 0.0
             ).astype(bf16)
+    for load in loads[5:]:
+        load.wait()
     elements = embed.shape[0]
     emb[...] = jnp.zeros_like(emb)
     emb[0:elements, :] = embed[...]
@@ -309,12 +325,12 @@
     ghosts = jnp.concatenate([tables[a].reshape(atoms, chans).T for a in range(3)], axis=1)
     picked[1] = own_pick + pick(ghosts, oh[atoms:, :])
     second = layer_out + forward(1)
-    x2 = dot3(rhid[...], second, (0, 0))
+    x2 = dot3(rhid[...], second, (1, 0))
     sig2 = sigmoid(x2)
     energy = jnp.sum(first_col * layer_out, axis=0, keepdims=True) + jnp.sum(
         last_col * (x2 * sig2), axis=0, keepdims=True
     )
-    d_second = dot3(rhid[...], last_col * (sig2 * (1.0 + x2 * (1.0 - sig2))), (1, 0))
+    d_second = dot3(rhid[...], last_col * (sig2 * (1.0 + x2 * (1.0 - sig2))), (0, 0))
     backward(1, d_second, True)
     d_ext = dot(oh[...], jnp.concatenate(split2(d_pick[...]), axis=0), (1, 1))
     d_ext = d_ext[:, :chans] + d_ext[:, chans:]
@@ -424,6 +440,10 @@
     structs = SLAB_STRUCTS * nx
     el_rows = -(-embed.shape[0] // 128) * 128
     grid = (2, 2, 2, per_cell, chans)
+    operands = (
+        positions, species[None], cell_map, neighbours, struct_ids[None], embed, w_up,
+        w_rad_in, w_rad_out, w_mix, read_first[None], read_hidden.T, read_last[None],
+    )
     dma = pltpu.SemaphoreType.DMA
     vm = lambda *shape: pltpu.VMEM(shape, f32)
     vmem = pl.BlockSpec(memory_space=pltpu.VMEM)
@@ -434,7 +454,7 @@
             jax.ShapeDtypeStruct((9, structs), f32),
             jax.ShapeDtypeStruct((3, atoms), f32),
         ),
-        in_specs=[vmem] * 13,
+        in_specs=[pl.BlockSpec(memory_space=pltpu.HBM)] * 13,
         out_specs=(vmem, vmem, vmem),
         scratch_shapes=[
             vm(-(-neigh // 8) * 8 + 8, atoms),
@@ -466,16 +486,15 @@
             vm(16, structs),
             vm(max(nx - 1, 1), 16, structs),
         ]
+        + [pltpu.VMEM(x.shape, x.dtype) for x in operands]
+        + [dma((13,))]
         + [dma((6,))] * 10
         + [dma((ny * nz - 1,))] * 2
         + [dma((max(nx - 1, 1),))] * 2,
         compiler_params=pltpu.CompilerParams(
             collective_id=0, has_side_effects=True, vmem_limit_bytes=48 * 1024 * 1024
         ),
-    )(
-        positions, species[None], cell_map, neighbours, struct_ids[None], embed, w_up,
-        w_rad_in, w_rad_out, w_mix, read_first[None], read_hidden, read_last[None],
-    )
+    )(*operands)
     return energies[0], virials, forces
 
 

time: 36.3 us -> 41.7 us (1.15)
  local copies, waits for them, and re-layouts: 5.38 us -> 10 us
  Pallas kernels: 29.9 us -> 30.7 us
    unnamed x28 -> x29, local copies, waits for them, and re-layouts: 5.38 us -> 10 us
    pallas_call x1, Pallas kernels: 29.9 us -> 30.7 us  [shards(): pl.pallas_call(functools.partial(kernel, counts), out_shape=(jax.ShapeDty...]
where the time goes in v1:
time: 41.7 us; the launch traced here: 41.3 us
  Pallas kernels  30.7 us (74%)
  local copies, waits for them, and re-layouts  10 us (24%)
  between operations  0.68 us (2%)
    pallas_call x1, Pallas kernels, shards(): pl.pallas_call(functools.partial(kernel, counts), out_shape=(jax.ShapeDty...  30.7 us
    unnamed x29, local copies, waits for them, and re-layouts  10 us

profile of v1, /device:TPU:0, one launch (start us, length us, event | category | flops | bytes accessed | tf_op | source)
XLA Modules:
  0.0 41.3 jit_solution(10549870604827930309)
XLA Ops:
  0.6 0.0 copy-start.4
  0.6 0.0 copy-start.8
  0.7 0.0 copy-start.9
  0.7 0.7 %copy-done.4 = f32[2,8,64]{2,1,0:T(8,128)S(1)} copy-done((f32[2,8,64]{2,1,0:T(8,128)S(1)}, f32[2,8,64]{2,1,0:T(8,128)}, u32[]{:S(2)}) %copy-start.4) | copy-done | bytes 4120
  1.3 0.0 copy-done.8
  1.3 0.0 copy-done.9
  1.3 0.0 copy-start
  1.3 1.0 %copy-done = f32[2,3,128,128]{3,2,1,0:T(8,128)S(1)} copy-done((f32[2,3,128,128]{3,2,1,0:T(8,128)S(1)}, f32[2,3,128,128]{3,2,1,0:T(8,128)}, u32[]{:S(2)}) %copy-start) | copy-done | bytes 393240
  2.3 0.0 copy-start.1
  2.3 0.9 %copy-done.1 = f32[2,128,128]{2,1,0:T(8,128)S(1)} copy-done((f32[2,128,128]{2,1,0:T(8,128)S(1)}, f32[2,128,128]{2,1,0:T(8,128)}, u32[]{:S(2)}) %copy-start.1) | copy-done | bytes 131096
  3.2 0.0 copy-start.2
  3.2 0.9 %copy-done.2 = f32[2,64,256]{2,1,0:T(8,128)S(1)} copy-done((f32[2,64,256]{2,1,0:T(8,128)S(1)}, f32[2,64,256]{2,1,0:T(8,128)}, u32[]{:S(2)}) %copy-start.2) | copy-done | bytes 131096
  4.1 0.0 copy-start.3
  4.1 0.8 %copy-done.3 = f32[89,128]{1,0:T(8,128)S(1)} copy-done((f32[89,128]{1,0:T(8,128)S(1)}, f32[89,128]{1,0:T(8,128)}, u32[]{:S(2)}) %copy-start.3) | copy-done | bytes 45592
  4.9 0.0 copy-start.5
  4.9 0.7 %copy-done.5 = f32[128,16]{0,1:T(8,128)S(1)} copy-done((f32[128,16]{0,1:T(8,128)S(1)}, f32[128,16]{0,1:T(8,128)}, u32[]{:S(2)}) %copy-start.5) | copy-done | bytes 8216
  5.6 0.0 copy-start.6
  5.6 0.7 %copy-done.6 = s32[8,128]{1,0:T(8,128)S(1)} copy-done((s32[8,128]{1,0:T(8,128)S(1)}, s32[8,128]{1,0:T(8,128)}, u32[]{:S(2)}) %copy-start.6) | copy-done | bytes 4120
  6.3 0.0 copy-start.7
  6.3 0.7 %copy-done.7 = f32[3,128]{1,0:T(4,128)S(1)} copy-done((f32[3,128]{1,0:T(4,128)S(1)}, f32[3,128]{1,0:T(4,128)}, u32[]{:S(2)}) %copy-start.7) | copy-done | bytes 1560
  7.0 0.0 copy-start.10
  7.0 0.7 %copy-done.10 = s32[128]{0:T(128)S(1)} copy-done((s32[128]{0:T(128)S(1)}, s32[128]{0:T(128)}, u32[]{:S(2)}) %copy-start.10) | copy-done | bytes 536
  7.7 0.0 copy-start.11
  7.7 0.7 %copy-done.11 = f32[128]{0:T(128)S(1)} copy-done((f32[128]{0:T(128)S(1)}, f32[128]{0:T(128)}, u32[]{:S(2)}) %copy-start.11) | copy-done | bytes 536
  8.3 0.0 copy-start.12
  8.3 0.7 %copy-done.12 = f32[16]{0:T(128)S(1)} copy-done((f32[16]{0:T(128)S(1)}, f32[16]{0:T(128)}, u32[]{:S(2)}) %copy-start.12) | copy-done | bytes 88
  9.0 30.7 %shard_map.148 = (f32[1,16]{1,0:T(1,128)S(1)}, f32[9,16]{1,0:T(8,128)S(1)}, f32[3,128]{1,0:T(4,128)S(1)}) custom-call(f32[3,128]{1,0:T(4,128)S(1)} %copy-done.7, s32[1,128]{1,0:T(1,128)S(1)} %bitcast.7, s32[1,128]{1,0:T(1,128)S(1)} %copy-done.9, s32[8,128]{1,0:T(8,128)S(1)} %copy-done.6, s32[1,128]{1,0:T(1,128)S(1)} %bitcast.8, f32[89,128]{1,0:T(8,128)S(1)} %copy-done.3, ...), custom_call_target="tpu_custom_call" | custom-call | tf_op jit(solution)/shard_map/pallas_call | solution.py:450
  39.6 0.5 %copy.19 = f32[16]{0:T(128)} copy(f32[16]{0:T(128)S(1)} %bitcast.11) | data formatting | bytes 128
  40.2 0.6 %copy.20 = f32[9,16]{1,0:T(8,128)} copy(f32[9,16]{1,0:T(8,128)S(1)} %get-tuple-element.13) | data formatting | bytes 1152
  40.8 0.6 %copy.21 = f32[3,128]{1,0:T(4,128)} copy(f32[3,128]{1,0:T(4,128)S(1)} %get-tuple-element.14) | data formatting | bytes 3072
Async XLA Ops:
  0.6 0.7 %copy-start.4 = (f32[2,8,64]{2,1,0:T(8,128)S(1)}, f32[2,8,64]{2,1,0:T(8,128)}, u32[]{:S(2)}) copy-start(f32[2,8,64]{2,1,0:T(8,128)} %refs_7_.1) | copy-start | bytes 12292
  0.6 0.7 %copy-start.8 = (s32[128]{0:T(128)S(1)}, s32[128]{0:T(128)}, u32[]{:S(2)}) copy-start(s32[128]{0:T(128)} %param.14) | copy-start | bytes 1540
  0.7 0.7 %copy-start.9 = (s32[1,128]{1,0:T(1,128)S(1)}, s32[1,128]{1,0:T(1,128)}, u32[]{:S(2)}) copy-start(s32[1,128]{1,0:T(1,128)} %refs_2_.1) | copy-start | bytes 1540
  1.3 1.0 %copy-start = (f32[2,3,128,128]{3,2,1,0:T(8,128)S(1)}, f32[2,3,128,128]{3,2,1,0:T(8,128)}, u32[]{:S(2)}) copy-start(f32[2,3,128,128]{3,2,1,0:T(8,128)} %refs_9_.1) | copy-start | bytes 1179652
  2.3 0.9 %copy-start.1 = (f32[2,128,128]{2,1,0:T(8,128)S(1)}, f32[2,128,128]{2,1,0:T(8,128)}, u32[]{:S(2)}) copy-start(f32[2,128,128]{2,1,0:T(8,128)} %refs_6_.1) | copy-start | bytes 393220
  3.2 0.9 %copy-start.2 = (f32[2,64,256]{2,1,0:T(8,128)S(1)}, f32[2,64,256]{2,1,0:T(8,128)}, u32[]{:S(2)}) copy-start(f32[2,64,256]{2,1,0:T(8,128)} %refs_8_.1) | copy-start | bytes 393220
  4.1 0.8 %copy-start.3 = (f32[89,128]{1,0:T(8,128)S(1)}, f32[89,128]{1,0:T(8,128)}, u32[]{:S(2)}) copy-start(f32[89,128]{1,0:T(8,128)} %refs_5_.1) | copy-start | bytes 136708
  4.9 0.7 %copy-start.5 = (f32[128,16]{0,1:T(8,128)S(1)}, f32[128,16]{0,1:T(8,128)}, u32[]{:S(2)}) copy-start(f32[128,16]{0,1:T(8,128)} %param.24) | copy-start | bytes 24580
  5.6 0.7 %copy-start.6 = (s32[8,128]{1,0:T(8,128)S(1)}, s32[8,128]{1,0:T(8,128)}, u32[]{:S(2)}) copy-start(s32[8,128]{1,0:T(8,128)} %refs_3_.1) | copy-start | bytes 12292
  6.3 0.7 %copy-start.7 = (f32[3,128]{1,0:T(4,128)S(1)}, f32[3,128]{1,0:T(4,128)}, u32[]{:S(2)}) copy-start(f32[3,128]{1,0:T(4,128)} %refs_0_.1) | copy-start | bytes 4612
  7.0 0.7 %copy-start.10 = (s32[128]{0:T(128)S(1)}, s32[128]{0:T(128)}, u32[]{:S(2)}) copy-start(s32[128]{0:T(128)} %param.17) | copy-start | bytes 1540
  7.7 0.7 %copy-start.11 = (f32[128]{0:T(128)S(1)}, f32[128]{0:T(128)}, u32[]{:S(2)}) copy-start(f32[128]{0:T(128)} %param.23) | copy-start | bytes 1540
  8.3 0.7 %copy-start.12 = (f32[16]{0:T(128)S(1)}, f32[16]{0:T(128)}, u32[]{:S(2)}) copy-start(f32[16]{0:T(128)} %param.25) | copy-start | bytes 196

commit v2 on v1

--- a/solution.py
+++ b/solution.py
@@ -90,7 +90,7 @@
 
 def run(
     counts, inputs,
-    en_out, vir_out, f_out,
+    packed,
     stage, emb, oh, soh, dirs, pre, rad, picked, grads, d_rad, d_pick, ddir, feats,
     sendp, sends, recvp, reccs, lsend, tables, back, backs, fsend, frecv, red, redstage,
     slab_buf, gx_send, gx_buf,
@@ -120,7 +120,11 @@
 
     slab_shifts = [(0, j, k) for j in range(ny) for k in range(nz) if (j, k) != (0, 0)]
     gx_shifts = [(i, 0, 0) for i in range(1, nx)]
-    peers = slab_shifts + gx_shifts
+    one_step = in_one_step(counts)
+    all_shifts = [
+        (i, j, k) for i in range(nx) for j in range(ny) for k in range(nz) if (i, j, k) != (0, 0, 0)
+    ]
+    peers = all_shifts if one_step else slab_shifts + gx_shifts
     barrier = pltpu.get_barrier_semaphore()
     for shift in peers:
         pl.semaphore_signal(barrier, inc=1, device_id=at(shift), device_id_type=MESH)
@@ -374,15 +378,24 @@
         redstage[3 * r : 3 * r + 3, :] = -over_slots(ev[r : r + 1] * eg)[0:3]
     redstage[9:10, :] = energy
     structs = SLAB_STRUCTS * nx
-    member = jnp.where(
-        lax.broadcasted_iota(jnp.int32, (structs, atoms), 0) == sid_c, 1.0, 0.0
-    ).astype(bf16)
-    shares = dot(parts3(redstage[...]).astype(bf16), member, (1, 1))
-    shares = shares[0:16] + shares[16:32] + shares[32:48]
-    red[...] = shares
-    my_slot = me["gy"] * nz + me["gz"]
+    if one_step:
+        slab_row = lax.broadcasted_iota(jnp.int32, (8, atoms), 0) + me["gx"] * SLAB_STRUCTS
+        local = jnp.where(slab_row == sid_c, 1.0, 0.0).astype(bf16)
+        shares = dot(local, parts3(redstage[...]).astype(bf16), (1, 1))
+        shares = shares[:, 0:16] + shares[:, 16:32] + shares[:, 32:48]
+        red[...] = shares[0:SLAB_STRUCTS]
+        my_slot = (me["gx"] * ny + me["gy"]) * nz + me["gz"]
+        first_shifts = all_shifts
+    else:
+        member = jnp.where(
+            lax.broadcasted_iota(jnp.int32, (structs, atoms), 0) == sid_c, 1.0, 0.0
+        ).astype(bf16)
+        shares = dot(parts3(redstage[...]).astype(bf16), member, (1, 1))
+        red[...] = shares[0:16] + shares[16:32] + shares[32:48]
+        my_slot = me["gy"] * nz + me["gz"]
+        first_shifts = slab_shifts
     sums = []
-    for i, shift in enumerate(slab_shifts):
+    for i, shift in enumerate(first_shifts):
         sums.append(remote(red, slab_buf.at[my_slot], a_s.at[i], a_r.at[i], shift))
     for copy in sums:
         copy.start()
@@ -400,17 +413,18 @@
         copy.start()
     own = spread[:, 0:atoms] - over_slots(eg)
     slab_buf[my_slot] = red[...]
-    for copy in sums:
-        copy.wait()
-    total = slab_buf[0]
-    for i in range(1, ny * nz):
-        total = total + slab_buf[i]
-    gx_send[...] = total
-    sums = []
-    for i, shift in enumerate(gx_shifts):
-        sums.append(remote(gx_send, gx_buf.at[i], g_s.at[i], g_r.at[i], shift))
-    for copy in sums:
-        copy.start()
+    if not one_step:
+        for copy in sums:
+            copy.wait()
+        total = slab_buf[0]
+        for i in range(1, ny * nz):
+            total = total + slab_buf[i]
+        gx_send[...] = total
+        sums = []
+        for i, shift in enumerate(gx_shifts):
+            sums.append(remote(gx_send, gx_buf.at[i], g_s.at[i], g_r.at[i], shift))
+        for copy in sums:
+            copy.start()
     for copy in copies:
         copy.wait()
     for axis in range(3):
@@ -418,13 +432,31 @@
     order = jnp.where(own_slot == iota1, 1.0, 0.0).astype(bf16)
     own3 = jnp.concatenate([parts3(-own), jnp.zeros_like(own)], axis=0).astype(bf16)
     forces = dot(own3, order, (1, 0))
-    f_out[...] = (forces[0:8] + forces[8:16] + forces[16:24])[0:3]
+    packed[16:19, 0:atoms] = (forces[0:8] + forces[8:16] + forces[16:24])[0:3]
     for copy in sums:
         copy.wait()
-    for i in range(len(gx_shifts)):
-        total = total + gx_buf[i]
-    vir_out[...] = total[0:9]
-    en_out[...] = total[9:10]
+    if one_step:
+        for g in range(nx):
+            total = slab_buf[g * ny * nz]
+            for i in range(1, ny * nz):
+                total = total + slab_buf[g * ny * nz + i]
+            gx_send[g * SLAB_STRUCTS : (g + 1) * SLAB_STRUCTS, :] = total
+        total = gx_send[...].T
+    else:
+        for i in range(len(gx_shifts)):
+            total = total + gx_buf[i]
+    packed[0:16, 0:structs] = total
+
+
+def in_one_step(counts):
+    return math.prod(counts) <= 64
+
+
+def unpack(packed, en_out, vir_out, f_out):
+    structs = en_out.shape[1]
+    en_out[...] = packed[9:10, 0:structs]
+    vir_out[...] = packed[0:9, 0:structs]
+    f_out[...] = packed[16:19, 0 : f_out.shape[1]]
 
 
 def shards(counts, *args):
@@ -444,18 +476,17 @@
         positions, species[None], cell_map, neighbours, struct_ids[None], embed, w_up,
         w_rad_in, w_rad_out, w_mix, read_first[None], read_hidden.T, read_last[None],
     )
+    one_step = in_one_step(counts)
+    share = (SLAB_STRUCTS, 16) if one_step else (16, structs)
+    groups = nx * ny * nz if one_step else ny * nz
     dma = pltpu.SemaphoreType.DMA
     vm = lambda *shape: pltpu.VMEM(shape, f32)
     vmem = pl.BlockSpec(memory_space=pltpu.VMEM)
-    energies, virials, forces = pl.pallas_call(
+    packed = pl.pallas_call(
         functools.partial(kernel, counts),
-        out_shape=(
-            jax.ShapeDtypeStruct((1, structs), f32),
-            jax.ShapeDtypeStruct((9, structs), f32),
-            jax.ShapeDtypeStruct((3, atoms), f32),
-        ),
+        out_shape=jax.ShapeDtypeStruct((24, max(atoms, structs)), f32),
         in_specs=[pl.BlockSpec(memory_space=pltpu.HBM)] * 13,
-        out_specs=(vmem, vmem, vmem),
+        out_specs=vmem,
         scratch_shapes=[
             vm(-(-neigh // 8) * 8 + 8, atoms),
             vm(el_rows, chans),
@@ -480,21 +511,32 @@
             vm(3, *grid),
             vm(3, 8, atoms),
             vm(6, 8, atoms),
-            vm(16, structs),
+            vm(*share),
             vm(16, atoms),
-            vm(ny * nz, 16, structs),
-            vm(16, structs),
+            vm(groups, *share),
+            vm(*((structs, 16) if one_step else share)),
             vm(max(nx - 1, 1), 16, structs),
         ]
         + [pltpu.VMEM(x.shape, x.dtype) for x in operands]
         + [dma((13,))]
         + [dma((6,))] * 10
-        + [dma((ny * nz - 1,))] * 2
+        + [dma((groups - 1,))] * 2
         + [dma((max(nx - 1, 1),))] * 2,
         compiler_params=pltpu.CompilerParams(
-            collective_id=0, has_side_effects=True, vmem_limit_bytes=48 * 1024 * 1024
+            collective_id=0, has_side_effects=True, vmem_limit_bytes=60 * 1024 * 1024
         ),
     )(*operands)
+    energies, virials, forces = pl.pallas_call(
+        unpack,
+        out_shape=(
+            jax.ShapeDtypeStruct((1, structs), f32),
+            jax.ShapeDtypeStruct((9, structs), f32),
+            jax.ShapeDtypeStruct((3, atoms), f32),
+        ),
+        in_specs=[vmem],
+        out_specs=(vmem, vmem, vmem),
+        compiler_params=pltpu.CompilerParams(vmem_limit_bytes=60 * 1024 * 1024),
+    )(packed)
     return energies[0], virials, forces
 
 

time: 41.7 us -> 32 us (0.77)
  local copies, waits for them, and re-layouts: 10 us -> 0 us
    unnamed x29 -> x0, local copies, waits for them, and re-layouts: 10 us -> none
    pallas_call x1 -> x2, Pallas kernels: 30.7 us -> 31.1 us  [the longest x1 29.8 us: shards(): pl.pallas_call(functools.partial(kernel, counts), out_shape=jax.ShapeDtyp...]
where the time goes in v2:
time: 32 us; the launch traced here: 31.8 us
  Pallas kernels  31.1 us (97%)
  between operations  0.64 us (2%)
    pallas_call x1, Pallas kernels, shards(): pl.pallas_call(functools.partial(kernel, counts), out_shape=jax.ShapeDtyp...  29.8 us
    pallas_call x1, Pallas kernels, shards(): pl.pallas_call(unpack, out_shape=(jax.ShapeDtypeStruct((1, structs), f32)...  1.31 us

profile of v2, /device:TPU:0, one launch (start us, length us, event | category | flops | bytes accessed | tf_op | source)
XLA Modules:
  0.0 31.8 jit_solution(16546350482305271268)
XLA Ops:
  0.6 29.8 %shard_map.148.packed = f32[24,128]{1,0:T(8,128)} custom-call(f32[3,128]{1,0:T(4,128)} %refs_0_.1, s32[1,128]{1,0:T(1,128)} %bitcast.7, s32[1,128]{1,0:T(1,128)} %refs_2_.1, s32[8,128]{1,0:T(8,128)} %refs_3_.1, s32[1,128]{1,0:T(1,128)} %bitcast.8, f32[89,128]{1,0:T(8,128)} %refs_5_.1, f32[2,128,128]{2,1,0:T(8,128)} %refs_6_.1, f32[2,8,64]{2,1,0:T(8,128)} %refs_7_.1, ...), custom_call_target="tpu_custom_call" | custom-call | tf_op jit(solution)/shard_map/pallas_call | solution.py:485
  30.5 1.3 %shard_map.149 = (f32[1,16]{1,0:T(1,128)}, f32[9,16]{1,0:T(8,128)}, f32[3,128]{1,0:T(4,128)}) custom-call(f32[24,128]{1,0:T(8,128)} %shard_map.148.packed), custom_call_target="tpu_custom_call" | custom-call | tf_op jit(solution)/shard_map/pallas_call | solution.py:529

commit v3 on v2

--- a/solution.py
+++ b/solution.py
@@ -336,10 +336,11 @@
     )
     d_second = dot3(rhid[...], last_col * (sig2 * (1.0 + x2 * (1.0 - sig2))), (0, 0))
     backward(1, d_second, True)
-    d_ext = dot(oh[...], jnp.concatenate(split2(d_pick[...]), axis=0), (1, 1))
+    d_both = jnp.concatenate(split2(d_pick[...]), axis=0)
+    d_ext = dot(oh[atoms:, :], d_both, (1, 1))
     d_ext = d_ext[:, :chans] + d_ext[:, chans:]
     for axis in range(3):
-        back[axis] = d_ext[(axis + 1) * atoms : (axis + 2) * atoms].reshape(grid)
+        back[axis] = d_ext[axis * atoms : (axis + 1) * atoms].reshape(grid)
     copies = []
     for axis in range(3):
         for side, step in ((1, -1), (0, 1)):
@@ -350,9 +351,10 @@
     for copy in copies:
         copy.start()
     d_bes = backward_radial(1)
+    d_own = dot(oh[0:atoms, :], d_both, (1, 1))
+    d_lifted = d_own[:, :chans] + d_own[:, chans:]
     for copy in copies:
         copy.wait()
-    d_lifted = d_ext[0:atoms]
     for axis in range(3):
         d_lifted = d_lifted + backs[axis].reshape(atoms, chans)
     d_layer = d_second + first_col + dot3(w_up[1], d_lifted, (1, 1))
@@ -366,6 +368,17 @@
     edge_row = lax.broadcasted_iota(jnp.int32, (8, edges), 0)
     eg = jnp.where(edge_row < 3, d_dir * inv + ev * (d_radius * inv), 0.0)
 
+    eg3 = jnp.concatenate([parts3(eg), jnp.zeros_like(eg)], axis=0).astype(bf16)
+    spread = dot(eg3, oh[...], (1, 1))
+    spread = spread[0:8] + spread[8:16] + spread[16:24]
+    for axis in range(3):
+        fsend[axis] = spread[:, (axis + 1) * atoms : (axis + 2) * atoms]
+    copies = []
+    for axis in range(3):
+        for face, step in ((2 * axis, -1), (2 * axis + 1, 1)):
+            copies.append(remote(fsend.at[axis], frecv.at[face], f_s.at[face], f_r.at[face], face_shift(axis, step)))
+    for copy in copies:
+        copy.start()
     redstage[...] = jnp.zeros_like(redstage)
 
     def over_slots(x):
@@ -400,17 +413,6 @@
     for copy in sums:
         copy.start()
 
-    eg3 = jnp.concatenate([parts3(eg), jnp.zeros_like(eg)], axis=0).astype(bf16)
-    spread = dot(eg3, oh[...], (1, 1))
-    spread = spread[0:8] + spread[8:16] + spread[16:24]
-    for axis in range(3):
-        fsend[axis] = spread[:, (axis + 1) * atoms : (axis + 2) * atoms]
-    copies = []
-    for axis in range(3):
-        for face, step in ((2 * axis, -1), (2 * axis + 1, 1)):
-            copies.append(remote(fsend.at[axis], frecv.at[face], f_s.at[face], f_r.at[face], face_shift(axis, step)))
-    for copy in copies:
-        copy.start()
     own = spread[:, 0:atoms] - over_slots(eg)
     slab_buf[my_slot] = red[...]
     if not one_step:

time: 32 us -> 31.6 us (0.988)
  Pallas kernels: 31.1 us -> 30.7 us
    pallas_call x1, Pallas kernels: 29.8 us -> 29.4 us  [shards(): pl.pallas_call(functools.partial(kernel, counts), out_shape=jax.ShapeDtyp...]
where the time goes in v3:
time: 31.6 us; the launch traced here: 31.3 us
  Pallas kernels  30.7 us (97%)
  between operations  0.64 us (2%)
    pallas_call x1, Pallas kernels, shards(): pl.pallas_call(functools.partial(kernel, counts), out_shape=jax.ShapeDtyp...  29.4 us
    pallas_call x1, Pallas kernels, shards(): pl.pallas_call(unpack, out_shape=(jax.ShapeDtypeStruct((1, structs), f32)...  1.31 us

profile of v3, /device:TPU:0, one launch (start us, length us, event | category | flops | bytes accessed | tf_op | source)
XLA Modules:
  0.0 31.3 jit_solution(9601835737238206788)
XLA Ops:
  0.6 29.4 %shard_map.148.packed = f32[24,128]{1,0:T(8,128)} custom-call(f32[3,128]{1,0:T(4,128)} %refs_0_.1, s32[1,128]{1,0:T(1,128)} %bitcast.7, s32[1,128]{1,0:T(1,128)} %refs_2_.1, s32[8,128]{1,0:T(8,128)} %refs_3_.1, s32[1,128]{1,0:T(1,128)} %bitcast.8, f32[89,128]{1,0:T(8,128)} %refs_5_.1, f32[2,128,128]{2,1,0:T(8,128)} %refs_6_.1, f32[2,8,64]{2,1,0:T(8,128)} %refs_7_.1, ...), custom_call_target="tpu_custom_call" | custom-call | tf_op jit(solution)/shard_map/pallas_call | solution.py:487
  30.0 1.3 %shard_map.149 = (f32[1,16]{1,0:T(1,128)}, f32[9,16]{1,0:T(8,128)}, f32[3,128]{1,0:T(4,128)}) custom-call(f32[24,128]{1,0:T(8,128)} %shard_map.148.packed), custom_call_target="tpu_custom_call" | custom-call | tf_op jit(solution)/shard_map/pallas_call | solution.py:531
